TPU v7x, 256 devices: a whole 4x4x8 slice. The times are simulated.
256 devices in a mesh: expert: 32 (over y, x, core), group: 8 (over z).
Axes of the slice: x: 4, y: 4, z: 8, core: 2. Of those that a mesh axis runs over, the one named last changes fastest.
Arguments:
- activations: bfloat16 [4096, 7168], P('expert', 'group'), may hold values from -6 to 6
- out_grads: bfloat16 [4096, 7168], P('expert', 'group'), may hold values from -6 to 6
- sketch_op: bfloat16 [7168, 128], P('group'), may hold values from -0.0625 to 0.0625
- block_lists: int32 [256, 32], P('expert'), may hold values from 0 to 31, as said below
- block_counts: int32 [256], P('expert'), may hold values from 1 to 32
- gate_values: bfloat16 [256, 32, 128], P('expert'), may hold values from 0.05 to 9, as said below
Outputs:
- basis_out: float32 [256, 7168, 128], P('expert', 'group')
Inputs may be any that keep to these rules, and one draw needn't show every extreme that they name: `block_lists`: each row is an ordering of all 32 block numbers, each once. `gate_values`: positive.
All inputs are finite; a program needn't handle non-finite values.
Results may differ from a plain program's by a relative error of at most 0.0042.
The roundings to bfloat16 on the way count: a program that leaves them out, or rounds other values in their place, can miss the bound.
Values may be sent and summed in bfloat16 or wider, within the bound.
No kernel may reach another device: no remote copies, remote signals or barrier semaphores. Data moves between devices by JAX's collectives and lax.ppermute only.
A program may use at most 64 MiB of HBM per device.

v0:
```python
import math
import jax
import jax.numpy as jnp
from jax import lax
from jax.sharding import PartitionSpec as P


def sketch_rows(rows_x, rows_y, weight_part):
    count_exp = weight_part.shape[0]
    row_count = rows_x.shape[0]
    sketch_rank = rows_y.shape[1]
    rows_wide = rows_y.astype(jnp.float32)
    contract = (((0,), (0,)), ((), ()))
    scaled = (weight_part.T[:, :, None] * rows_wide[:, None, :]).astype(jnp.bfloat16)
    scaled = scaled.reshape(row_count, count_exp * sketch_rank)
    return lax.dot_general(rows_x, scaled, contract, preferred_element_type=jnp.float32)


def gram_of(sketch_flat, sketch_rank):
    shaped = sketch_flat.reshape(sketch_flat.shape[0], -1, sketch_rank)
    return jnp.einsum("dkr,dks->rs", shaped, shaped, precision=lax.Precision.HIGHEST)


def on_device(activations, out_grads, sketch_op, block_lists, block_counts, gate_values):
    sketch_rank = sketch_op.shape[1]
    feat_width = activations.shape[1]
    local_exp = block_lists.shape[0]
    blocks = block_lists.shape[1]
    partial_sketch = jnp.dot(out_grads, sketch_op, preferred_element_type=jnp.float32)
    sketched = lax.psum(partial_sketch, "group").astype(jnp.bfloat16)
    slot_ids = jnp.arange(blocks, dtype=jnp.int32)
    slot_live = slot_ids[None, :] < block_counts[:, None]
    onehot = ((block_lists[:, :, None] == slot_ids[None, None, :]) & slot_live[:, :, None]).astype(
        jnp.float32
    )
    weights = jnp.einsum("ejb,ejt->ebt", onehot, gate_values.astype(jnp.float32)).reshape(
        local_exp, -1
    )
    piece_rows = lax.all_gather(activations, "expert", axis=0, tiled=True)
    piece_sketch = lax.all_gather(sketched, "expert", axis=0, tiled=True)
    sketch_all = sketch_rows(piece_rows, piece_sketch, weights)
    gram_total = lax.psum(gram_of(sketch_all, sketch_rank), ("expert", "group"))
    factor = jnp.linalg.cholesky(gram_total)
    stacked = (
        sketch_all.reshape(feat_width, local_exp, sketch_rank)
        .transpose(1, 0, 2)
        .reshape(-1, sketch_rank)
    )
    basis_flat = lax.linalg.triangular_solve(
        factor, stacked, left_side=False, lower=True, transpose_a=True
    )
    out_scale = math.sqrt(local_exp * lax.axis_size("expert") * feat_width * lax.axis_size("group"))
    return (basis_flat * out_scale).reshape(local_exp, feat_width, sketch_rank)


def solution(mesh):
    in_specs = (
        P("expert", "group"),
        P("expert", "group"),
        P("group", None),
        P("expert", None),
        P("expert"),
        P("expert", None, None),
    )
    out_specs = P("expert", "group", None)
    return jax.shard_map(
        on_device, mesh=mesh, in_specs=in_specs, out_specs=out_specs, check_vma=False
    )
```

profile of v0, /device:TPU:1, one launch (start us, length us, event | category | flops | bytes accessed | tf_op | source)
XLA Modules:
  0.0 443.5 jit_solution(5734964180359648877)
XLA Ops:
  6.5 0.0 copy-start
  6.5 0.0 all-gather.3.cloned.1.call-start
  6.5 0.9 copy-done
  7.5 1.1 fusion.10
  8.6 27.5 %psum.14 = bf16[128,128]{1,0:T(8,128)(2,1)} all-reduce(f32[128,128]{1,0:T(8,128)S(1)} %fusion.10), channel_id=1, replica_groups=mesh['expert'=32,'group'=8] {'group'}, use_global_device_ids=true, to_apply=%region_0.0 | all-reduce | flops 16384 | bytes 98304 | tf_op jit(solution)/shard_map/psum | solution.py:30
  36.2 0.0 all-gather.3.cloned.1.call-update
  36.2 0.0 all-gather.5.cloned.1.call-start
  36.2 0.7 all-gather.5.cloned.1.call-update
  36.9 0.0 all-reduce.2.cloned.1.call-start
  37.0 0.7 iota_compare_fusion.3
  37.7 1.0 convolution_bitcast_fusion
  38.7 0.1 copy.26
  38.8 0.6 copy.11
  39.4 50.1 %all-gather.3.cloned.1.call-done = bf16[4096,128]{1,0:T(8,128)(2,1)} async-done(((bf16[128,128]{1,0:T(8,128)(2,1)}), bf16[4096,128]{1,0:T(8,128)(2,1)}) %all-gather.3.cloned.1.call-update) | async-done | bytes 1048592 | tf_op jit(solution)/shard_map/all_gather | solution.py:40
  89.5 1.4 convert_element_type.16
  90.9 16.4 %multiply_convert_fusion = bf16[4096,8,128]{2,1,0:T(8,128)(2,1)} fusion(f32[4096,128]{1,0:T(8,128)S(1)} %convert_element_type.16, f32[4096,8]{1,0:T(8,128)S(1)} %copy.11), kind=kLoop, calls=%fused_computation | loop fusion | flops 8388608 | bytes 10616832 | tf_op jit(solution)/shard_map/convert_element_type | solution.py:14
  107.2 40.0 %all-gather.5.cloned.1.call-done = bf16[4096,896]{1,0:T(8,128)(2,1)} async-done(((bf16[128,896]{1,0:T(8,128)(2,1)}), bf16[4096,896]{1,0:T(8,128)(2,1)}) %all-gather.5.cloned.1.call-update) | async-done | bytes 7340048 | tf_op jit(solution)/shard_map/all_gather | solution.py:39
  147.3 12.9 %fusion = f32[1024,896]{1,0:T(8,128)S(1)} fusion(bf16[4096,896]{1,0:T(8,128)(2,1)} %all-gather.5.cloned.1.call-done, bf16[512,8,8,128]{3,2,1,0:T(8,128)(2,1)} %bitcast.40), kind=kOutput, calls=%fused_computation.2 | convolution fusion | flops 7516192768 | bytes 19398656 | tf_op jit(solution)/shard_map/dot_general | solution.py:16
  160.2 0.0 copy-start.1
  160.2 1.8 copy-done.1
  162.1 3.6 convolution_bitcast_fusion.1
  165.7 0.0 all-reduce.2.cloned.1.call-update
  165.7 5.0 %copy.12 = f32[896,8,128]{2,0,1:T(8,128)} copy(f32[896,8,128]{0,2,1:T(8,128)} %bitcast.38) | data formatting | bytes 7340032 | tf_op jit(solution)/shard_map/reshape | solution.py:45
  170.7 235.7 %all-reduce.2.cloned.1.call-done = f32[128,128]{0,1:T(8,128)} async-done(((f32[128,128]{0,1:T(8,128)}), f32[128,128]{0,1:T(8,128)}) %all-reduce.2.cloned.1.call-update) | async-done | bytes 65552 | tf_op jit(solution)/shard_map/psum | solution.py:42
  406.4 0.9 copy.15
  407.4 0.9 fusion.7
  408.2 11.7 %cholesky.16 = f32[128,128]{1,0:T(8,128)S(1)} custom-call(f32[128,128]{1,0:T(8,128)S(1)} %fusion.7), custom_call_target="Cholesky" | custom-call | tf_op jit(solution)/shard_map/jit(cholesky)/cholesky | solution.py:43
  420.0 0.6 compare_reduce_fusion
  420.6 0.7 fusion.5
  421.3 9.8 %custom-call.6 = f32[1,128,128]{1,2,0:T(8,128)S(1)} custom-call(f32[1,128,128]{2,1,0:T(8,128)S(1)} %fusion.5), custom_call_target="InvertDiagBlocksLowerTriangular" | custom-call | tf_op jit(solution)/shard_map/triangular_solve | solution.py:49
  431.1 5.9 %convolution_multiply_fusion = f32[7168,128]{1,0:T(8,128)} fusion(f32[7168,128]{1,0:T(8,128)} %bitcast.39, f32[1,128,128]{1,2,0:T(8,128)S(1)} %custom-call.6), kind=kOutput, calls=%fused_computation.1 | convolution fusion | flops 1410203648 | bytes 7405568 | tf_op jit(solution)/shard_map/triangular_solve | solution.py:49
  (1 shorter events, 0.0 us)
Async XLA Ops:
  6.5 0.9 copy-start
  6.5 83.0 %all-gather.3.cloned.1.call-start = ((), (), s32[]{:S(2)}) async-start(), calls=%async_computation | async-start | bytes 1081344 | tf_op jit(solution)/shard_map/all_gather | solution.py:40
  36.2 111.1 %all-gather.5.cloned.1.call-start = ((), (), s32[]{:S(2)}) async-start(), calls=%async_computation.1 | async-start | bytes 7569408 | tf_op jit(solution)/shard_map/all_gather | solution.py:39
  36.9 369.5 %all-reduce.2.cloned.1.call-start = ((), (), s32[]{:S(2)}) async-start(), calls=%async_computation.2 | async-start | bytes 131072 | tf_op jit(solution)/shard_map/psum | solution.py:42
  160.2 1.8 copy-start.1
Sparse Core Ops, SparseCore 0:
  36.3 53.1 all-gather.2
  92.0 55.1 all-gather.4
  165.8 240.5 all-reduce.1
where the time goes:
time: 444 us
  waiting for transfers between devices  327 us (74%)
  other arithmetic  42.2 us (10%)
  blocking collectives  27.5 us (6%)
  matrix products  24.7 us (6%)
  between operations  13.2 us (3%)
  local copies, waits for them, and re-layouts  9.39 us (2%)
    psum x1, waiting for transfers between devices, on_device(): gram_total = lax.psum(gram_of(sketch_all, sketch_rank), ('expert', 'group'))  236 us
    all_gather x1, waiting for transfers between devices, on_device(): piece_sketch = lax.all_gather(sketched, 'expert', axis=0, tiled=True)  50.1 us
    all_gather x1, waiting for transfers between devices, on_device(): piece_rows = lax.all_gather(activations, 'expert', axis=0, tiled=True)  40 us
    psum x1, blocking collectives, on_device(): sketched = lax.psum(partial_sketch, 'group').astype(jnp.bfloat16)  27.5 us
    convert_element_type x1, other arithmetic, sketch_rows(): (weight_part.T[:, :, None] * rows_wide[:, None, :]).astype(jnp.bfloat16)  16.4 us
    dot_general x1, matrix products, sketch_rows(): lax.dot_general(rows_x, scaled, contract, preferred_element_type=jnp.floa...  12.9 us
    another operation x3, other arithmetic, on_device(): factor = jnp.linalg.cholesky(gram_total)  12.4 us
    another operation x2, other arithmetic, on_device(): lax.linalg.triangular_solve(factor, stacked, left_side=False, lower=True,...  10.5 us
  transfers between devices with their start and end apart: 3, of which 3 were waited for; matrix products, arithmetic and copies ran while one was open for 6% of the time, Pallas kernels for 0%

commit v1 on v0

--- a/solution.py
+++ b/solution.py
@@ -37,7 +37,9 @@
         local_exp, -1
     )
     piece_rows = lax.all_gather(activations, "expert", axis=0, tiled=True)
-    piece_sketch = lax.all_gather(sketched, "expert", axis=0, tiled=True)
+    piece_sketch = jnp.concatenate(
+        lax.all_to_all(jnp.stack([sketched] * lax.axis_size("expert")), "expert", 0, 0), axis=0
+    )
     sketch_all = sketch_rows(piece_rows, piece_sketch, weights)
     gram_total = lax.psum(gram_of(sketch_all, sketch_rank), ("expert", "group"))
     factor = jnp.linalg.cholesky(gram_total)

time: 444 us -> 389 us (0.88)
  waiting for transfers between devices: 327 us -> 259 us
  starting transfers between devices: 0.08 us -> 14.1 us
    all_gather x1 -> x0, waiting for transfers between devices: 50.1 us -> none  [on_device(): piece_sketch = lax.all_gather(sketched, 'expert', axis=0, tiled=True)]
    all_gather x1, waiting for transfers between devices: 40 us -> 0.01 us  [on_device(): piece_rows = lax.all_gather(activations, 'expert', axis=0, tiled=True)]
    all_to_all x0 -> x1, waiting for transfers between devices: none -> 25.3 us  [on_device(): lax.all_to_all(jnp.stack([sketched] * lax.axis_size('expert')), 'expert',...]
    all_to_all x0 -> x1, starting transfers between devices: none -> 14 us  [on_device(): lax.all_to_all(jnp.stack([sketched] * lax.axis_size('expert')), 'expert',...]
  transfers between devices with their start and end apart: 3 -> 3, of which waited for: 3 -> 2; matrix products, arithmetic and copies ran while one was open for 6% -> 6% of each run, Pallas kernels for 0% -> 0%
where the time goes in v1:
time: 389 us; the launch traced here: 388 us
  waiting for transfers between devices  259 us (67%)
  other arithmetic  40.4 us (10%)
  blocking collectives  27.8 us (7%)
  matrix products  23.8 us (6%)
  starting transfers between devices  14.1 us (4%)
  between operations  13.5 us (3%)
  local copies, waits for them, and re-layouts  9.87 us (3%)
    psum x1, waiting for transfers between devices, on_device(): gram_total = lax.psum(gram_of(sketch_all, sketch_rank), ('expert', 'group'))  233 us
    psum x1, blocking collectives, on_device(): sketched = lax.psum(partial_sketch, 'group').astype(jnp.bfloat16)  27.8 us
    all_to_all x1, waiting for transfers between devices, on_device(): lax.all_to_all(jnp.stack([sketched] * lax.axis_size('expert')), 'expert',...  25.3 us
    convert_element_type x1, other arithmetic, sketch_rows(): (weight_part.T[:, :, None] * rows_wide[:, None, :]).astype(jnp.bfloat16)  16.4 us
    all_to_all x1, starting transfers between devices, on_device(): lax.all_to_all(jnp.stack([sketched] * lax.axis_size('expert')), 'expert',...  14 us
    dot_general x1, matrix products, sketch_rows(): lax.dot_general(rows_x, scaled, contract, preferred_element_type=jnp.floa...  13 us
    another operation x3, other arithmetic, on_device(): factor = jnp.linalg.cholesky(gram_total)  12.4 us
    another operation x2, other arithmetic, on_device(): lax.linalg.triangular_solve(factor, stacked, left_side=False, lower=True,...  10.5 us
  transfers between devices with their start and end apart: 3, of which 2 were waited for; matrix products, arithmetic and copies ran while one was open for 6% of the time, Pallas kernels for 0%

profile of v1, /device:TPU:1, one launch (start us, length us, event | category | flops | bytes accessed | tf_op | source)
XLA Modules:
  0.0 388.5 jit_solution(4507928852008643385)
XLA Ops:
  6.5 0.0 copy-start
  6.5 0.0 all-gather.2.cloned.1.call-start
  6.6 0.7 all-gather.2.cloned.1.call-update
  7.3 0.2 copy-done
  7.5 1.1 fusion.10
  8.6 27.8 %psum.14 = bf16[128,128]{1,0:T(8,128)(2,1)S(1)} all-reduce(f32[128,128]{1,0:T(8,128)S(1)} %fusion.10), channel_id=1, replica_groups=mesh['expert'=32,'group'=8] {'group'}, use_global_device_ids=true, to_apply=%region_0.0 | all-reduce | flops 16384 | bytes 98304 | tf_op jit(solution)/shard_map/psum | solution.py:30
  36.4 1.2 stack.2
  37.6 14.0 %all-to-all-start = ((bf16[32,128,128]{2,1,0:T(8,128)(2,1)}), bf16[32,128,128]{2,1,0:T(8,128)(2,1)S(1)}, u32[]{:S(2)}, u32[]{:S(2)}) async-start(bf16[32,128,128]{2,1,0:T(8,128)(2,1)} %stack.2), calls=%async_computation | async-start | bytes 2097152 | tf_op jit(solution)/shard_map/all_to_all | solution.py:41
  51.6 0.0 all-reduce.2.cloned.1.call-start
  51.7 0.0 copy-done.4
  51.7 0.1 iota_compare_fusion.3
  51.8 0.0 copy-done.2
  51.8 0.1 convolution_bitcast_fusion
  51.9 0.1 copy.26
  52.0 0.6 copy.11
  52.6 25.3 %all-to-all-done = bf16[32,128,128]{2,1,0:T(8,128)(2,1)S(1)} async-done(((bf16[32,128,128]{2,1,0:T(8,128)(2,1)}), bf16[32,128,128]{2,1,0:T(8,128)(2,1)S(1)}, u32[]{:S(2)}, u32[]{:S(2)}) %all-to-all-start) | async-done | bytes 1048608 | tf_op jit(solution)/shard_map/all_to_all | solution.py:41
  77.9 0.2 bitcast_convert_fusion
  78.1 16.4 %multiply_convert_fusion = bf16[4096,8,128]{2,1,0:T(8,128)(2,1)} fusion(f32[4096,128]{1,0:T(8,128)S(1)} %bitcast_convert_fusion, f32[4096,8]{1,0:T(8,128)S(1)} %copy.11), kind=kLoop, calls=%fused_computation | loop fusion | flops 8388608 | bytes 10616832 | tf_op jit(solution)/shard_map/convert_element_type | solution.py:14
  94.5 13.0 %fusion = f32[1024,896]{1,0:T(8,128)S(1)} fusion(bf16[4096,896]{1,0:T(8,128)(2,1)} %all-gather.2.cloned.1.call-done, bf16[512,8,8,128]{3,2,1,0:T(8,128)(2,1)} %bitcast.43), kind=kOutput, calls=%fused_computation.2 | convolution fusion | flops 7516192768 | bytes 19398656 | tf_op jit(solution)/shard_map/dot_general | solution.py:16
  107.4 0.0 copy-start.1
  107.4 1.8 copy-done.1
  109.3 3.6 convolution_bitcast_fusion.1
  112.9 0.0 all-reduce.2.cloned.1.call-update
  112.9 5.0 %copy.12 = f32[896,8,128]{2,0,1:T(8,128)} copy(f32[896,8,128]{0,2,1:T(8,128)} %bitcast.41) | data formatting | bytes 7340032 | tf_op jit(solution)/shard_map/reshape | solution.py:47
  117.9 233.1 %all-reduce.2.cloned.1.call-done = f32[128,128]{0,1:T(8,128)} async-done(((f32[128,128]{0,1:T(8,128)}), f32[128,128]{0,1:T(8,128)}) %all-reduce.2.cloned.1.call-update) | async-done | bytes 65552 | tf_op jit(solution)/shard_map/psum | solution.py:44
  351.1 0.9 copy.15
  352.0 0.9 fusion.7
  352.9 11.7 %cholesky.16 = f32[128,128]{1,0:T(8,128)S(1)} custom-call(f32[128,128]{1,0:T(8,128)S(1)} %fusion.7), custom_call_target="Cholesky" | custom-call | tf_op jit(solution)/shard_map/jit(cholesky)/cholesky | solution.py:45
  364.6 0.6 compare_reduce_fusion
  365.3 0.7 fusion.5
  365.9 9.8 %custom-call.6 = f32[1,128,128]{1,2,0:T(8,128)S(1)} custom-call(f32[1,128,128]{2,1,0:T(8,128)S(1)} %fusion.5), custom_call_target="InvertDiagBlocksLowerTriangular" | custom-call | tf_op jit(solution)/shard_map/triangular_solve | solution.py:51
  375.7 5.9 %convolution_multiply_fusion = f32[7168,128]{1,0:T(8,128)} fusion(f32[7168,128]{1,0:T(8,128)} %bitcast.42, f32[1,128,128]{1,2,0:T(8,128)S(1)} %custom-call.6), kind=kOutput, calls=%fused_computation.1 | convolution fusion | flops 1410203648 | bytes 7405568 | tf_op jit(solution)/shard_map/triangular_solve | solution.py:51
  (6 shorter events, 0.0 us)
Async XLA Ops:
  6.5 0.9 copy-start
  6.5 45.1 %copy-start.4 = (s32[8]{0:T(128)S(1)}, s32[8]{0:T(128)}, u32[]{:S(2)}) copy-start(s32[8]{0:T(128)} %param.10) | copy-start | bytes 100
  6.5 45.2 %copy-start.2 = (bf16[8,32,128]{2,1,0:T(8,128)(2,1)S(1)}, bf16[8,32,128]{2,1,0:T(8,128)(2,1)}, u32[]{:S(2)}) copy-start(bf16[8,32,128]{2,1,0:T(8,128)(2,1)} %param.11) | copy-start | bytes 196612
  6.5 45.2 %copy-start.3 = (s32[8,32]{1,0:T(8,128)S(1)}, s32[8,32]{1,0:T(8,128)}, u32[]{:S(2)}) copy-start(s32[8,32]{1,0:T(8,128)} %param.9) | copy-start | bytes 3076
  6.5 87.9 %all-gather.2.cloned.1.call-start = ((), (), s32[]{:S(2)}) async-start(), calls=%async_computation.1 | async-start | bytes 7569408 | tf_op jit(solution)/shard_map/all_gather | solution.py:39
  37.6 40.3 %all-to-all-start = ((bf16[32,128,128]{2,1,0:T(8,128)(2,1)}), bf16[32,128,128]{2,1,0:T(8,128)(2,1)S(1)}, u32[]{:S(2)}, u32[]{:S(2)}) async-start(bf16[32,128,128]{2,1,0:T(8,128)(2,1)} %stack.2), calls=%async_computation | async-start | bytes 2097152 | tf_op jit(solution)/shard_map/all_to_all | solution.py:41
  51.6 299.4 %all-reduce.2.cloned.1.call-start = ((), (), s32[]{:S(2)}) async-start(), calls=%async_computation.2 | async-start | bytes 131072 | tf_op jit(solution)/shard_map/psum | solution.py:44
  107.4 1.8 copy-start.1
Sparse Core Ops, SparseCore 0:
  9.9 70.5 all-gather.1
  113.1 237.9 all-reduce.1
